TPU v7x, 512 devices: a whole 4x8x8 slice. The times are simulated.
512 devices in a mesh: region: 4 (over z_lo), group: 16 (over z_hi, y), loop: 8 (over x, core).
Axes of the slice: x: 4, y: 8, z: 8 (z_hi: 2, z_lo: 4; z = z_hi * 4 + z_lo), core: 2. Of those that a mesh axis runs over, the one named last changes fastest.
Arguments:
- history: float32 [16, 262144], P(None, ('region', 'group', 'loop')), may hold values from -6 to 6
- incident: float32 [4, 262144], P(None, ('region', 'group', 'loop')), may hold values from -6 to 6
- positions: float32 [3, 262144], P(None, ('region', 'group', 'loop')), may hold values from -1 to 1
- area: float32 [262144], P(('region', 'group', 'loop')), may hold values from 0.00390625 to 0.03125
- self_weight: float32 [262144], P(('region', 'group', 'loop')), may hold values from 1 to 2
- pair_target: int32 [512, 24], P(('region', 'group', 'loop')), may hold values from 0 to 31
- pair_source: int32 [512, 24], P(('region', 'group', 'loop')), may hold values from 0 to 7
- pair_lag: int32 [512, 24], P(('region', 'group', 'loop')), may hold values from 1 to 12
- pair_count: int32 [512], P(('region', 'group', 'loop')), may hold values from 16 to 24, as said below
- junc_send: int32 [512, 128], P(('region', 'group', 'loop')), may hold values from 0 to 511
- junc_recv: int32 [512, 128], P(('region', 'group', 'loop')), may hold values from 0 to 511
- junc_gain: float32 [512, 128], P(('region', 'group', 'loop')), may hold values from 0.5 to 2
- adjacency: int32 [512], P(('region', 'group', 'loop')), may hold values from 1 to 3
Outputs:
- density: float32 [4, 262144], P(None, ('region', 'group', 'loop'))
Inputs may be any that keep to these rules, and one draw needn't show every extreme that they name: `pair_count`: each device uses between 16 and 24 of its listed pairs, and some device uses all 24.
All inputs are finite; a program needn't handle non-finite values.
Results may differ from a plain program's by a relative error of at most 0.0003.
Values sent between devices are 32-bit elements; how exact they have to be, the bound alone decides.
No kernel may reach another device: no remote copies, remote signals or barrier semaphores. Data moves between devices by JAX's collectives and lax.ppermute only.
A program may use at most 64 MiB of HBM per device.

v0:
```python
import jax
import jax.numpy as jnp
from jax import lax
from jax.sharding import PartitionSpec as P

HIST = 16
STEPS = 4
soften = 0.25


def spline_mix(frac, rows):
    one_minus = 1.0 - frac
    cube = frac * frac * frac
    square = frac * frac
    first = one_minus * one_minus * one_minus / 6.0
    second = (3.0 * cube - 6.0 * square + 4.0) / 6.0
    third = (-3.0 * cube + 3.0 * square + 3.0 * frac + 1.0) / 6.0
    fourth = cube / 6.0
    return (
        first * rows[3][None, :]
        + second * rows[2][None, :]
        + third * rows[1][None, :]
        + fourth * rows[0][None, :]
    )


def pair_term(target_pos, source_pos, source_area, rows):
    delta = target_pos[:, :, None] - source_pos[:, None, :]
    dist_sq = jnp.sum(delta * delta, axis=0)
    weight = source_area[None, :] * lax.rsqrt(dist_sq + soften)
    frac = dist_sq / (1.0 + dist_sq)
    return jnp.sum(weight * spline_mix(frac, rows), axis=1)


def body(
    history,
    incident,
    positions,
    area,
    self_weight,
    pair_target,
    pair_source,
    pair_lag,
    pair_count,
    junc_send,
    junc_recv,
    junc_gain,
    adjacency,
):
    node_dev = history.shape[1]
    tile_rows = node_dev // 2
    groups = lax.axis_size("group")
    regions = lax.axis_size("region")
    target_pos = lax.all_gather(positions, "group", axis=1, tiled=True)
    source_pos, source_area = (
        lax.all_gather(positions, "loop", axis=1, tiled=True),
        lax.all_gather(area, "loop", axis=0, tiled=True),
    )
    stored = jnp.concatenate([history, jnp.zeros((STEPS, node_dev), jnp.float32)], axis=0)
    partner = (lax.axis_index("region") + adjacency[0]) % regions
    zero = jnp.zeros((), jnp.int32)
    outputs = []
    for step in range(STEPS):
        seen_history = lax.all_gather(stored, "loop", axis=1, tiled=True)

        def pair_fn(index, acc):
            target_row = pair_target[0, index] * tile_rows
            source_row = pair_source[0, index] * node_dev
            start = HIST + step - pair_lag[0, index] - 3
            tile_pos = lax.dynamic_slice(target_pos, (zero, target_row), (3, tile_rows))
            member_pos = lax.dynamic_slice(source_pos, (zero, source_row), (3, node_dev))
            member_area = lax.dynamic_slice(source_area, (source_row,), (node_dev,))
            rows = lax.dynamic_slice(seen_history, (start, source_row), (4, node_dev))
            term = pair_term(tile_pos, member_pos, member_area, rows)
            current = lax.dynamic_slice(acc, (target_row,), (tile_rows,))
            return lax.dynamic_update_slice(acc, current + term, (target_row,))

        partial_value = lax.fori_loop(
            0, pair_count[0], pair_fn, jnp.zeros((groups * node_dev,), jnp.float32)
        )
        field = lax.psum_scatter(partial_value, "group", scatter_dimension=0, tiled=True)
        trace = stored[HIST + step - 1][junc_send[0]]
        traces = lax.all_gather(trace[None, :], "region", axis=0, tiled=True)
        received = lax.dynamic_index_in_dim(traces, partner, 0, keepdims=False)
        junction = jnp.zeros((node_dev,), jnp.float32).at[junc_recv[0]].add(junc_gain[0] * received)
        density_now = (incident[step] - field - junction) / self_weight
        stored = stored.at[HIST + step].set(density_now)
        outputs.append(density_now)
    return jnp.stack(outputs, axis=0)


def solution(mesh):
    in_specs = (
        P(None, ("region", "group", "loop")),
        P(None, ("region", "group", "loop")),
        P(None, ("region", "group", "loop")),
        P(("region", "group", "loop")),
        P(("region", "group", "loop")),
        P(("region", "group", "loop"), None),
        P(("region", "group", "loop"), None),
        P(("region", "group", "loop"), None),
        P(("region", "group", "loop")),
        P(("region", "group", "loop"), None),
        P(("region", "group", "loop"), None),
        P(("region", "group", "loop"), None),
        P(("region", "group", "loop")),
    )
    out_specs = P(None, ("region", "group", "loop"))
    return jax.shard_map(body, mesh=mesh, in_specs=in_specs, out_specs=out_specs, check_vma=False)
```

profile of v0, /device:TPU:64, one launch (start us, length us, event | category | flops | bytes accessed | tf_op | source)
XLA Modules:
  0.0 1410.5 jit_solution(5847321745746539040)
XLA Ops:
  1.4 0.7 slice.208
  2.1 1.3 gather_fusion
  3.4 12.7 all-gather.5
  16.1 1.4 scatter_custom_fusion
  17.6 52.4 %all_gather.34 = f32[3,8192]{1,0:T(4,128)S(1)} all-gather(f32[3,512]{1,0:T(4,128)S(1)} %copy-done.4), channel_id=1, replica_groups=mesh['region'=4,'group'=16,'loop'=8] {'group'}, dimensions={1}, use_global_device_ids=true | all-gather | bytes 104448 | tf_op jit(solution)/shard_map/all_gather | solution.py:54
  70.0 13.1 all_gather.35
  83.1 11.3 all-gather.4
  94.4 13.0 all_gather.36
  107.4 152.6 %while.59 = (s32[]{:T(128)}, f32[8192]{0:T(1024)S(1)}, s32[]{:T(128)}, s32[1,24]{1,0:T(1,128)S(1)}, s32[1,24]{1,0:T(1,128)S(1)}, /*index=5*/f32[4096]{0:T(1024)S...) while((s32[]{:T(128)}, f32[8192]{0:T(1024)S(1)}, ...), condition=%wide.region_3.4_spmd, body=%wide.region_0.3_spmd.sunk | while | flops 4720660 | bytes 1111457 | solution.py:78
  112.7 0.7 fusion.112
  121.7 0.7 fusion.112
  130.6 0.7 fusion.112
  260.0 141.7 %all-reduce.1 = f32[8192]{0:T(1024)S(1)} all-reduce(f32[8192]{0:T(1024)S(1)} %get-tuple-element.853), channel_id=6, replica_groups=mesh['region'=4,'group'=16,'loop'=8] {'group'}, use_global_device_ids=true, to_apply=%region_4.5.clone | all-reduce | flops 8192 | bytes 65536
  401.6 1.3 dynamic-slice.28
  403.7 23.8 %all_gather.38 = f32[20,4096]{1,0:T(8,128)S(1)} all-gather(f32[20,512]{1,0:T(8,128)S(1)} %scatter.10), channel_id=1, replica_groups=mesh['region'=4,'group'=16,'loop'=8] {'loop'}, dimensions={1}, use_global_device_ids=true | all-gather | bytes 368640 | tf_op jit(solution)/shard_map/all_gather | solution.py:64
  427.5 152.5 %while.60 = (s32[]{:T(128)}, f32[8192]{0:T(1024)S(1)}, s32[]{:T(128)}, s32[1,24]{1,0:T(1,128)S(1)}, s32[1,24]{1,0:T(1,128)S(1)}, /*index=5*/f32[4096]{0:T(1024)S...) while((s32[]{:T(128)}, f32[8192]{0:T(1024)S(1)}, ...), condition=%wide.region_9.10_spmd, body=%wide.region_6.9_spmd.sunk | while | flops 4720660 | bytes 1111457 | solution.py:78
  580.0 141.7 %all-reduce.2 = f32[8192]{0:T(1024)S(1)} all-reduce(f32[8192]{0:T(1024)S(1)} %get-tuple-element.854), channel_id=7, replica_groups=mesh['region'=4,'group'=16,'loop'=8] {'group'}, use_global_device_ids=true, to_apply=%region_10.11.clone | all-reduce | flops 8192 | bytes 65536
  721.7 1.3 gather_fusion.1
  723.0 24.4 %all-gather.6 = f32[4,1,128]{2,1,0:T(1,128)S(1)} all-gather(f32[1,1,128]{2,1,0:T(1,128)S(1)} %bitcast.187), channel_id=3, replica_groups=mesh['region'=4,'group'=16,'loop'=8] {'region'}, dimensions={0}, use_global_device_ids=true | all-gather | bytes 2560 | tf_op jit(solution)/shard_map/all_gather | solution.py:83
  747.4 1.4 scatter_custom_fusion.1
  748.9 13.0 all_gather.40
  761.9 152.5 %while.61 = (s32[]{:T(128)}, f32[8192]{0:T(1024)S(1)}, s32[]{:T(128)}, s32[1,24]{1,0:T(1,128)S(1)}, s32[1,24]{1,0:T(1,128)S(1)}, /*index=5*/f32[4096]{0:T(1024)S...) while((s32[]{:T(128)}, f32[8192]{0:T(1024)S(1)}, ...), condition=%wide.region_15.16_spmd, body=%wide.region_12.15_spmd.sunk | while | flops 4720660 | bytes 1111457 | solution.py:78
  914.4 141.7 %all-reduce.3 = f32[8192]{0:T(1024)S(1)} all-reduce(f32[8192]{0:T(1024)S(1)} %get-tuple-element.855), channel_id=8, replica_groups=mesh['region'=4,'group'=16,'loop'=8] {'group'}, use_global_device_ids=true, to_apply=%region_16.17.clone | all-reduce | flops 8192 | bytes 65536
  1056.1 1.3 gather_fusion.2
  1057.4 19.6 %all-gather.7 = f32[4,1,128]{2,1,0:T(1,128)S(1)} all-gather(f32[1,1,128]{2,1,0:T(1,128)S(1)} %bitcast.188), channel_id=4, replica_groups=mesh['region'=4,'group'=16,'loop'=8] {'region'}, dimensions={0}, use_global_device_ids=true | all-gather | bytes 2560 | tf_op jit(solution)/shard_map/all_gather | solution.py:83
  1076.9 1.4 scatter_custom_fusion.2
  1078.5 13.0 all_gather.42
  1091.5 152.7 %while.62 = (s32[]{:T(128)}, f32[8192]{0:T(1024)S(1)}, s32[]{:T(128)}, s32[1,24]{1,0:T(1,128)S(1)}, s32[1,24]{1,0:T(1,128)S(1)}, /*index=5*/f32[4096]{0:T(1024)S...) while((s32[]{:T(128)}, f32[8192]{0:T(1024)S(1)}, ...), condition=%wide.region_21.22_spmd, body=%wide.region_18.21_spmd.sunk | while | flops 4720660 | bytes 1111457 | solution.py:78
  1244.1 141.7 %all-reduce.4 = f32[8192]{0:T(1024)S(1)} all-reduce(f32[8192]{0:T(1024)S(1)} %get-tuple-element.856), channel_id=9, replica_groups=mesh['region'=4,'group'=16,'loop'=8] {'group'}, use_global_device_ids=true, to_apply=%region_22.23.clone | all-reduce | flops 8192 | bytes 65536
  1385.8 1.3 gather_fusion.3
  1387.1 21.3 %all-gather.8 = f32[4,1,128]{2,1,0:T(1,128)S(1)} all-gather(f32[1,1,128]{2,1,0:T(1,128)S(1)} %bitcast.186), channel_id=5, replica_groups=mesh['region'=4,'group'=16,'loop'=8] {'region'}, dimensions={0}, use_global_device_ids=true | all-gather | bytes 2560 | tf_op jit(solution)/shard_map/all_gather | solution.py:83
  1408.4 1.4 scatter_custom_fusion.3
  (650 shorter events, 172.2 us)
Async XLA Ops:
  0.0 94.4 %copy-start.3 = (f32[16,512]{1,0:T(8,128)S(1)}, f32[16,512]{1,0:T(8,128)}, u32[]{:S(2)}) copy-start(f32[16,512]{1,0:T(8,128)} %param.27) | copy-start | bytes 98308
  0.0 16.1 %copy-start.7 = (f32[1,128]{1,0:T(1,128)S(1)}, f32[1,128]{1,0:T(1,128)}, u32[]{:S(2)}) copy-start(f32[1,128]{1,0:T(1,128)} %param.38) | copy-start | bytes 1540
  0.0 16.1 %copy-start.9 = (s32[1,128]{1,0:T(1,128)S(1)}, s32[1,128]{1,0:T(1,128)}, u32[]{:S(2)}) copy-start(s32[1,128]{1,0:T(1,128)} %param.37) | copy-start | bytes 1540
  0.0 17.6 %copy-start.4 = (f32[3,512]{1,0:T(4,128)S(1)}, f32[3,512]{1,0:T(4,128)}, u32[]{:S(2)}) copy-start(f32[3,512]{1,0:T(4,128)} %param.29) | copy-start | bytes 18436
  0.0 83.1 %copy-start.8 = (f32[512]{0:T(512)S(1)}, f32[512]{0:T(512)}, u32[]{:S(2)}) copy-start(f32[512]{0:T(512)} %param.30) | copy-start | bytes 6148
  3.4 103.9 %copy-start = (s32[1,24]{1,0:T(1,128)S(1)}, s32[1,24]{1,0:T(1,128)}, u32[]{:S(2)}) copy-start(s32[1,24]{1,0:T(1,128)} %param.32) | copy-start | bytes 292
  3.4 103.9 %copy-start.1 = (s32[1,24]{1,0:T(1,128)S(1)}, s32[1,24]{1,0:T(1,128)}, u32[]{:S(2)}) copy-start(s32[1,24]{1,0:T(1,128)} %param.33) | copy-start | bytes 292
  3.4 103.9 %copy-start.2 = (s32[1,24]{1,0:T(1,128)S(1)}, s32[1,24]{1,0:T(1,128)}, u32[]{:S(2)}) copy-start(s32[1,24]{1,0:T(1,128)} %param.34) | copy-start | bytes 292
  107.4 296.2 %copy-start.6 = (f32[4,512]{1,0:T(4,128)S(1)}, f32[4,512]{1,0:T(4,128)}, u32[]{:S(2)}) copy-start(f32[4,512]{1,0:T(4,128)} %param.28) | copy-start | bytes 24580
  107.4 296.2 %copy-start.5 = (f32[512]{0:T(512)S(1)}, f32[512]{0:T(512)}, u32[]{:S(2)}) copy-start(f32[512]{0:T(512)} %param.31) | copy-start | bytes 6148
where the time goes:
time: 1420 us; the launch traced here: 1410 us
  blocking collectives  784 us (55%)
  loops' own time  438 us (31%)
  other arithmetic  173 us (12%)
    unnamed x4, blocking collectives  567 us
    another operation x4, loops' own time, body(): lax.fori_loop(0, pair_count[0], pair_fn, jnp.zeros((groups * node_dev,),...  438 us
    all_gather x4, blocking collectives, body(): traces = lax.all_gather(trace[None, :], 'region', axis=0, tiled=True)  77.9 us
    all_gather x4, blocking collectives, body(): seen_history = lax.all_gather(stored, 'loop', axis=1, tiled=True)  62.7 us
    all_gather x1, blocking collectives, body(): target_pos = lax.all_gather(positions, 'group', axis=1, tiled=True)  52.4 us
    sub x68, other arithmetic, pair_fn(): start = HIST + step - pair_lag[0, index] - 3  45.7 us
    mul x68, other arithmetic, pair_fn(): target_row = pair_target[0, index] * tile_rows  45.5 us
    reduce_sum x68, other arithmetic, pair_term(): return jnp.sum(weight * spline_mix(frac, rows), axis=1)  40.8 us

commit v1 on v0

--- a/solution.py
+++ b/solution.py
@@ -1,11 +1,22 @@
+import functools
 import jax
 import jax.numpy as jnp
 from jax import lax
 from jax.sharding import PartitionSpec as P
+from jax.lax import all_to_all, axis_size
 
 HIST = 16
 STEPS = 4
 soften = 0.25
+
+
+def run_quarters(local, peer_axis):
+    return jnp.concatenate(
+        all_to_all(jnp.stack([local] * axis_size(peer_axis), axis=0), peer_axis, 0, 0), axis=0
+    )
+
+
+form_column_in = functools.partial(run_quarters, peer_axis="region")
 
 
 def spline_mix(frac, rows):
@@ -80,7 +91,7 @@
         )
         field = lax.psum_scatter(partial_value, "group", scatter_dimension=0, tiled=True)
         trace = stored[HIST + step - 1][junc_send[0]]
-        traces = lax.all_gather(trace[None, :], "region", axis=0, tiled=True)
+        traces = form_column_in(trace[None, :])
         received = lax.dynamic_index_in_dim(traces, partner, 0, keepdims=False)
         junction = jnp.zeros((node_dev,), jnp.float32).at[junc_recv[0]].add(junc_gain[0] * received)
         density_now = (incident[step] - field - junction) / self_weight

time: 1420 us -> 1400 us (0.986)
  the two profiles are of different devices: /device:TPU:64 before, /device:TPU:6 now
where the time goes in v1:
time: 1400 us; the launch traced here: 1390 us
  loops' own time  616 us (44%)
  blocking collectives  495 us (35%)
  other arithmetic  234 us (17%)
  starting transfers between devices  22.8 us (2%)
  local copies, waits for them, and re-layouts  19 us (1%)
    another operation x4, loops' own time, body(): lax.fori_loop(0, pair_count[0], pair_fn, jnp.zeros((groups * node_dev,),...  616 us
    unnamed x4, blocking collectives  364 us
    sub x96, other arithmetic, pair_fn(): start = HIST + step - pair_lag[0, index] - 3  60.7 us
    mul x96, other arithmetic, pair_fn(): target_row = pair_target[0, index] * tile_rows  60.7 us
    reduce_sum x96, other arithmetic, pair_term(): return jnp.sum(weight * spline_mix(frac, rows), axis=1)  57.6 us
    all_gather x1, blocking collectives, body(): target_pos = lax.all_gather(positions, 'group', axis=1, tiled=True)  55 us
    all_gather x4, blocking collectives, body(): seen_history = lax.all_gather(stored, 'loop', axis=1, tiled=True)  52.1 us
  transfers between devices with their start and end apart: 4, of which 0 were waited for; matrix products, arithmetic and copies ran while one was open for 4% of the time, Pallas kernels for 0%

profile of v1, /device:TPU:6, one launch (start us, length us, event | category | flops | bytes accessed | tf_op | source)
XLA Modules:
  0.0 1388.5 jit_solution(9254736690736510465)
XLA Ops:
  0.0 0.7 fusion.81
  0.7 0.7 slice.208
  1.4 1.3 gather_fusion
  3.3 7.3 all-to-all-start
  10.6 55.0 %all_gather.22 = f32[3,8192]{1,0:T(4,128)S(1)} all-gather(f32[3,512]{1,0:T(4,128)S(1)} %copy-done.4), channel_id=1, replica_groups=mesh['region'=4,'group'=16,'loop'=8] {'group'}, dimensions={1}, use_global_device_ids=true | all-gather | bytes 104448 | tf_op jit(solution)/shard_map/all_gather | solution.py:65
  65.6 12.8 all_gather.23
  78.4 11.1 all-gather
  89.4 13.0 all_gather.24
  102.5 215.1 %while.59 = (s32[]{:T(128)}, f32[8192]{0:T(1024)S(1)}, s32[]{:T(128)}, s32[1,24]{1,0:T(1,128)S(1)}, s32[1,24]{1,0:T(1,128)S(1)}, /*index=5*/f32[4096]{0:T(1024)S...) while((s32[]{:T(128)}, f32[8192]{0:T(1024)S(1)}, ...), condition=%wide.region_3.4_spmd, body=%wide.region_0.3_spmd.sunk | while | flops 4720660 | bytes 1111457 | solution.py:89
  107.8 0.7 fusion.108
  125.7 0.7 fusion.108
  317.6 91.1 %all-reduce.1 = f32[8192]{0:T(1024)S(1)} all-reduce(f32[8192]{0:T(1024)S(1)} %get-tuple-element.853), channel_id=2, replica_groups=mesh['region'=4,'group'=16,'loop'=8] {'group'}, use_global_device_ids=true, to_apply=%region_4.5.clone | all-reduce | flops 8192 | bytes 65536
  409.3 1.3 dynamic-slice.28
  411.4 1.4 scatter_custom_fusion
  412.9 1.3 gather_fusion.1
  414.2 13.0 all_gather.25
  427.2 216.1 %while.60 = (s32[]{:T(128)}, f32[8192]{0:T(1024)S(1)}, s32[]{:T(128)}, s32[1,24]{1,0:T(1,128)S(1)}, s32[1,24]{1,0:T(1,128)S(1)}, /*index=5*/f32[4096]{0:T(1024)S...) while((s32[]{:T(128)}, f32[8192]{0:T(1024)S(1)}, ...), condition=%wide.region_9.10_spmd, body=%wide.region_6.9_spmd.sunk | while | flops 4720660 | bytes 1111457 | solution.py:89
  643.9 5.1 all-to-all-start.1
  649.0 91.1 %all-reduce.2 = f32[8192]{0:T(1024)S(1)} all-reduce(f32[8192]{0:T(1024)S(1)} %get-tuple-element.854), channel_id=3, replica_groups=mesh['region'=4,'group'=16,'loop'=8] {'group'}, use_global_device_ids=true, to_apply=%region_10.11.clone | all-reduce | flops 8192 | bytes 65536
  740.1 1.4 scatter_custom_fusion.1
  741.6 1.3 gather_fusion.2
  743.0 13.0 all_gather.26
  755.9 214.6 %while.61 = (s32[]{:T(128)}, f32[8192]{0:T(1024)S(1)}, s32[]{:T(128)}, s32[1,24]{1,0:T(1,128)S(1)}, s32[1,24]{1,0:T(1,128)S(1)}, /*index=5*/f32[4096]{0:T(1024)S...) while((s32[]{:T(128)}, f32[8192]{0:T(1024)S(1)}, ...), condition=%wide.region_15.16_spmd, body=%wide.region_12.15_spmd.sunk | while | flops 4720660 | bytes 1111457 | solution.py:89
  971.1 5.3 all-to-all-start.2
  976.4 91.1 %all-reduce.3 = f32[8192]{0:T(1024)S(1)} all-reduce(f32[8192]{0:T(1024)S(1)} %get-tuple-element.855), channel_id=4, replica_groups=mesh['region'=4,'group'=16,'loop'=8] {'group'}, use_global_device_ids=true, to_apply=%region_16.17.clone | all-reduce | flops 8192 | bytes 65536
  1067.5 1.4 scatter_custom_fusion.2
  1069.0 1.3 gather_fusion.3
  1070.4 13.2 all_gather.27
  1083.5 206.1 %while.62 = (s32[]{:T(128)}, f32[8192]{0:T(1024)S(1)}, s32[]{:T(128)}, s32[1,24]{1,0:T(1,128)S(1)}, s32[1,24]{1,0:T(1,128)S(1)}, /*index=5*/f32[4096]{0:T(1024)S...) while((s32[]{:T(128)}, f32[8192]{0:T(1024)S(1)}, ...), condition=%wide.region_21.22_spmd, body=%wide.region_18.21_spmd.sunk | while | flops 4720660 | bytes 1111457 | solution.py:89
  1290.2 5.1 all-to-all-start.3
  1295.3 91.1 %all-reduce.4 = f32[8192]{0:T(1024)S(1)} all-reduce(f32[8192]{0:T(1024)S(1)} %get-tuple-element.856), channel_id=5, replica_groups=mesh['region'=4,'group'=16,'loop'=8] {'group'}, use_global_device_ids=true, to_apply=%region_22.23.clone | all-reduce | flops 8192 | bytes 65536
  1386.4 1.4 scatter_custom_fusion.3
  (910 shorter events, 238.4 us)
Async XLA Ops:
  0.0 89.4 %copy-start.3 = (f32[16,512]{1,0:T(8,128)S(1)}, f32[16,512]{1,0:T(8,128)}, u32[]{:S(2)}) copy-start(f32[16,512]{1,0:T(8,128)} %param.27) | copy-start | bytes 98308
  0.0 10.6 copy-start.4
  0.0 78.4 %copy-start.9 = (s32[1,128]{1,0:T(1,128)S(1)}, s32[1,128]{1,0:T(1,128)}, u32[]{:S(2)}) copy-start(s32[1,128]{1,0:T(1,128)} %param.37) | copy-start | bytes 1540
  0.0 78.4 %copy-start.8 = (f32[512]{0:T(512)S(1)}, f32[512]{0:T(512)}, u32[]{:S(2)}) copy-start(f32[512]{0:T(512)} %param.30) | copy-start | bytes 6148
  2.7 99.7 %copy-start = (s32[1,24]{1,0:T(1,128)S(1)}, s32[1,24]{1,0:T(1,128)}, u32[]{:S(2)}) copy-start(s32[1,24]{1,0:T(1,128)} %param.32) | copy-start | bytes 292
  2.7 99.7 %copy-start.1 = (s32[1,24]{1,0:T(1,128)S(1)}, s32[1,24]{1,0:T(1,128)}, u32[]{:S(2)}) copy-start(s32[1,24]{1,0:T(1,128)} %param.33) | copy-start | bytes 292
  2.7 99.7 %copy-start.2 = (s32[1,24]{1,0:T(1,128)S(1)}, s32[1,24]{1,0:T(1,128)}, u32[]{:S(2)}) copy-start(s32[1,24]{1,0:T(1,128)} %param.34) | copy-start | bytes 292
  3.3 408.0 %all-to-all-start = ((f32[4,1,128]{2,1,0:T(1,128)}), f32[4,1,128]{2,1,0:T(1,128)S(1)}, u32[]{:S(2)}, u32[]{:S(2)}) async-start(f32[4,1,128]{2,1,0:T(1,128)} %stack.27), calls=%async_computation | async-start | bytes 4096 | tf_op jit(solution)/shard_map/all_to_all | solution.py:15
  102.4 215.1 %copy-start.6 = (f32[4,512]{1,0:T(4,128)S(1)}, f32[4,512]{1,0:T(4,128)}, u32[]{:S(2)}) copy-start(f32[4,512]{1,0:T(4,128)} %param.28) | copy-start | bytes 24580
  102.4 308.9 %copy-start.7 = (f32[1,128]{1,0:T(1,128)S(1)}, f32[1,128]{1,0:T(1,128)}, u32[]{:S(2)}) copy-start(f32[1,128]{1,0:T(1,128)} %param.38) | copy-start | bytes 1540
  102.5 310.3 %copy-start.5 = (f32[512]{0:T(512)S(1)}, f32[512]{0:T(512)}, u32[]{:S(2)}) copy-start(f32[512]{0:T(512)} %param.31) | copy-start | bytes 6148
  643.9 96.2 %all-to-all-start.1 = ((f32[4,1,128]{2,1,0:T(1,128)}), f32[4,1,128]{2,1,0:T(1,128)S(1)}, u32[]{:S(2)}, u32[]{:S(2)}) async-start(f32[4,1,128]{2,1,0:T(1,128)} %stack.29), calls=%async_computation.1 | async-start | bytes 4096 | tf_op jit(solution)/shard_map/all_to_all | solution.py:15
  971.1 96.4 %all-to-all-start.2 = ((f32[4,1,128]{2,1,0:T(1,128)}), f32[4,1,128]{2,1,0:T(1,128)S(1)}, u32[]{:S(2)}, u32[]{:S(2)}) async-start(f32[4,1,128]{2,1,0:T(1,128)} %stack.31), calls=%async_computation.2 | async-start | bytes 4096 | tf_op jit(solution)/shard_map/all_to_all | solution.py:15
  1290.2 96.2 %all-to-all-start.3 = ((f32[4,1,128]{2,1,0:T(1,128)}), f32[4,1,128]{2,1,0:T(1,128)S(1)}, u32[]{:S(2)}, u32[]{:S(2)}) async-start(f32[4,1,128]{2,1,0:T(1,128)} %stack.33), calls=%async_computation.3 | async-start | bytes 4096 | tf_op jit(solution)/shard_map/all_to_all | solution.py:15
